TPU v7x, 32 devices: a whole 2x2x4 slice. The times are simulated.
32 devices in a mesh: rep: 16 (over z, x, core), shard: 2 (over y).
Axes of the slice: x: 2, y: 2, z: 4, core: 2. Of those that a mesh axis runs over, the one named last changes fastest.
Arguments:
- tokens: bfloat16 [4096, 1024], P(('rep', 'shard')), may hold values from -6 to 6
- lengths: int32 [32], P(('rep', 'shard')), may hold values from 32 to 128, as said below
- qkv_weight: bfloat16 [1024, 3072], P('shard'), may hold values from -0.1875 to 0.1875
- query_bias: bfloat16 [1024], P('shard'), may hold values from -3 to 3
- value_bias: bfloat16 [1024], P('shard'), may hold values from -3 to 3
- proj_weight: bfloat16 [1024, 1024], P('shard'), may hold values from -0.5 to 0.5
- proj_bias: bfloat16 [1024], P('shard'), may hold values from -3 to 3
- attn_gain: bfloat16 [1024], P('shard'), may hold values from 0.5 to 1.5
- attn_shift: bfloat16 [1024], P('shard'), may hold values from -3 to 3
- up_weight: bfloat16 [1024, 4096], P('shard'), may hold values from -0.1875 to 0.1875
- up_bias: bfloat16 [4096], P('shard'), may hold values from -3 to 3
- down_weight: bfloat16 [4096, 1024], P('shard'), may hold values from -0.09375 to 0.09375
- down_bias: bfloat16 [1024], P('shard'), may hold values from -3 to 3
- ffn_gain: bfloat16 [1024], P('shard'), may hold values from 0.5 to 1.5
- ffn_shift: bfloat16 [1024], P('shard'), may hold values from -3 to 3
- cotangent: bfloat16 [4096, 1024], P(('rep', 'shard')), may hold values from -6 to 6
Outputs:
- layer_output: bfloat16 [4096, 1024], P(('rep', 'shard'))
- grad_tokens: bfloat16 [4096, 1024], P(('rep', 'shard'))
- grad_qkv_weight: float32 [1024, 3072], P('shard')
- grad_query_bias: float32 [1024], P('shard')
- grad_value_bias: float32 [1024], P('shard')
- grad_proj_weight: float32 [1024, 1024], P('shard')
- grad_proj_bias: float32 [1024], P('shard')
- grad_attn_gain: float32 [1024], P('shard')
- grad_attn_shift: float32 [1024], P('shard')
- grad_up_weight: float32 [1024, 4096], P('shard')
- grad_up_bias: float32 [4096], P('shard')
- grad_down_weight: float32 [4096, 1024], P('shard')
- grad_down_bias: float32 [1024], P('shard')
- grad_ffn_gain: float32 [1024], P('shard')
- grad_ffn_shift: float32 [1024], P('shard')
Inputs may be any that keep to these rules, and one draw needn't show every extreme that they name: `lengths`: every sequence has at least one quarter of its 128 tokens valid; some sequence is whole and some has exactly 32 valid tokens.
All inputs are finite; a program needn't handle non-finite values.
Results may differ from a plain program's by a relative error of at most 0.018.
Values may be sent and summed in bfloat16 or wider, within the bound.
No kernel may reach another device: no remote copies, remote signals or barrier semaphores. Data moves between devices by JAX's collectives and lax.ppermute only.
A program may use at most 192 MiB of HBM per device.

v0:
```python
import jax
import jax.numpy as jnp
from jax import lax
from jax.sharding import PartitionSpec as P

HEADS = 16
HEAD_DIM = 64
LEN = 128
EPSILON = 1e-05
SQRT_HALF = 0.7071067811865476
INV_ROOT_TAU = 0.3989422804014327


def gelu_value(pre_act):
    return 0.5 * pre_act * (1.0 + lax.erf(pre_act * SQRT_HALF))


def gelu_slope(pre_act):
    return 0.5 * (1.0 + lax.erf(pre_act * SQRT_HALF)) + pre_act * INV_ROOT_TAU * jnp.exp(
        -0.5 * pre_act * pre_act
    )


def layer_norm(hidden):
    centred = hidden - jnp.mean(hidden, axis=-1, keepdims=True)
    inverse = lax.rsqrt(jnp.mean(centred * centred, axis=-1, keepdims=True) + EPSILON)
    return (centred * inverse, inverse)


def norm_backward(upstream, normed, inverse, gain):
    scaled = upstream * gain
    return inverse * (
        scaled
        - jnp.mean(scaled, axis=-1, keepdims=True)
        - normed * jnp.mean(scaled * normed, axis=-1, keepdims=True)
    )


def contract_rows(former, latter):
    return lax.dot_general(
        former, latter, (((0,), (0,)), ((), ())), preferred_element_type=jnp.float32
    )


def times_transposed(former, latter):
    return lax.dot_general(
        former, latter, (((1,), (1,)), ((), ())), preferred_element_type=jnp.float32
    )


def split_heads(matrix):
    return matrix.reshape(matrix.shape[0] // LEN, LEN, HEADS, HEAD_DIM)


def merge_heads(tensor):
    return tensor.reshape(tensor.shape[0] * LEN, HEADS * HEAD_DIM)


def score_block(query_rows, key_rows, lengths):
    scores = jnp.einsum(
        "sqhd,skhd->shqk",
        split_heads(query_rows),
        split_heads(key_rows),
        preferred_element_type=jnp.float32,
    ) * HEAD_DIM ** (-0.5)
    positions = jnp.arange(LEN, dtype=jnp.int32)
    usable = (positions[None, :] < lengths[:, None])[:, None, None, :]
    return (scores, usable)


def attention_backward(query_rows, key_rows, value_rows, log_total, lengths, grad_context):
    scores, usable = score_block(query_rows, key_rows, lengths)
    exact = jnp.where(usable, jnp.exp(scores - log_total), 0.0)
    shares = exact.astype(jnp.bfloat16)
    context_heads = split_heads(grad_context)
    grad_value = jnp.einsum(
        "shqk,sqhd->skhd", shares, context_heads, preferred_element_type=jnp.float32
    )
    grad_shares = jnp.einsum(
        "sqhd,skhd->shqk",
        context_heads,
        split_heads(value_rows),
        preferred_element_type=jnp.float32,
    )
    grad_scores = (
        exact
        * (grad_shares - jnp.sum(exact * grad_shares, axis=-1, keepdims=True))
        * HEAD_DIM ** (-0.5)
    ).astype(jnp.bfloat16)
    grad_query = jnp.einsum(
        "shqk,skhd->sqhd", grad_scores, split_heads(key_rows), preferred_element_type=jnp.float32
    )
    grad_key = jnp.einsum(
        "shqk,sqhd->skhd", grad_scores, split_heads(query_rows), preferred_element_type=jnp.float32
    )
    return (merge_heads(grad_query), merge_heads(grad_key), merge_heads(grad_value))


def per_device(
    tokens,
    lengths,
    qkv_weight,
    query_bias,
    value_bias,
    proj_weight,
    proj_bias,
    attn_gain,
    attn_shift,
    up_weight,
    up_bias,
    down_weight,
    down_bias,
    ffn_gain,
    ffn_shift,
    cotangent,
):
    qkv_full, query_full, value_full, proj_full, proj_bias_full, attn_gain_full, attn_shift_full = (
        lax.all_gather(qkv_weight, "shard", axis=0, tiled=True),
        lax.all_gather(query_bias, "shard", axis=0, tiled=True),
        lax.all_gather(value_bias, "shard", axis=0, tiled=True),
        lax.all_gather(proj_weight, "shard", axis=0, tiled=True),
        lax.all_gather(proj_bias, "shard", axis=0, tiled=True),
        lax.all_gather(attn_gain, "shard", axis=0, tiled=True),
        lax.all_gather(attn_shift, "shard", axis=0, tiled=True),
    )
    model_width = tokens.shape[1]
    project = jnp.dot(tokens, qkv_full, preferred_element_type=jnp.float32)
    query_rows = (project[:, :model_width] + query_full.astype(jnp.float32)).astype(jnp.bfloat16)
    key_rows = project[:, model_width : 2 * model_width].astype(jnp.bfloat16)
    value_rows = (project[:, 2 * model_width :] + value_full.astype(jnp.float32)).astype(
        jnp.bfloat16
    )
    scores, usable = score_block(query_rows, key_rows, lengths)
    log_total = jnp.log(jnp.sum(jnp.where(usable, jnp.exp(scores), 0.0), axis=-1, keepdims=True))
    shares = jnp.where(usable, jnp.exp(scores - log_total), 0.0).astype(jnp.bfloat16)
    context = merge_heads(
        jnp.einsum(
            "shqk,skhd->sqhd", shares, split_heads(value_rows), preferred_element_type=jnp.float32
        )
    ).astype(jnp.bfloat16)
    attn_sum = (
        tokens.astype(jnp.float32)
        + jnp.dot(context, proj_full, preferred_element_type=jnp.float32)
        + proj_bias_full.astype(jnp.float32)
    )
    normed_one, inverse_one = layer_norm(attn_sum)
    mid_state = normed_one * attn_gain_full.astype(jnp.float32) + attn_shift_full.astype(
        jnp.float32
    )
    mid_half = mid_state.astype(jnp.bfloat16)
    up_full, up_bias_full, down_full, down_bias_full, ffn_gain_full, ffn_shift_full = (
        lax.all_gather(up_weight, "shard", axis=0, tiled=True),
        lax.all_gather(up_bias, "shard", axis=0, tiled=True),
        lax.all_gather(down_weight, "shard", axis=0, tiled=True),
        lax.all_gather(down_bias, "shard", axis=0, tiled=True),
        lax.all_gather(ffn_gain, "shard", axis=0, tiled=True),
        lax.all_gather(ffn_shift, "shard", axis=0, tiled=True),
    )
    pre_act = jnp.dot(mid_half, up_full, preferred_element_type=jnp.float32) + up_bias_full.astype(
        jnp.float32
    )
    hidden = gelu_value(pre_act).astype(jnp.bfloat16)
    ffn_sum = (
        mid_state
        + jnp.dot(hidden, down_full, preferred_element_type=jnp.float32)
        + down_bias_full.astype(jnp.float32)
    )
    normed_two, inverse_two = layer_norm(ffn_sum)
    layer_output = (
        normed_two * ffn_gain_full.astype(jnp.float32) + ffn_shift_full.astype(jnp.float32)
    ).astype(jnp.bfloat16)
    token_cols, context_cols, mid_cols, hidden_cols = (
        lax.all_to_all(tokens, "shard", split_axis=1, concat_axis=0, tiled=True),
        lax.all_to_all(context, "shard", split_axis=1, concat_axis=0, tiled=True),
        lax.all_to_all(mid_half, "shard", split_axis=1, concat_axis=0, tiled=True),
        lax.all_to_all(hidden, "shard", split_axis=1, concat_axis=0, tiled=True),
    )
    upstream = cotangent.astype(jnp.float32)
    grad_ffn_shift = jnp.sum(upstream, axis=0)
    grad_ffn_gain = jnp.sum(upstream * normed_two, axis=0)
    grad_ffn_sum = norm_backward(
        upstream, normed_two, inverse_two, ffn_gain_full.astype(jnp.float32)
    )
    ffn_half = grad_ffn_sum.astype(jnp.bfloat16)
    grad_down_bias = jnp.sum(grad_ffn_sum, axis=0)
    grad_pre = times_transposed(ffn_half, down_full) * gelu_slope(pre_act)
    pre_half = grad_pre.astype(jnp.bfloat16)
    grad_up_bias = jnp.sum(grad_pre, axis=0)
    grad_mid = grad_ffn_sum + times_transposed(pre_half, up_full)
    pre_group, ffn_group = (
        lax.all_gather(pre_half, "shard", axis=0, tiled=True),
        lax.all_gather(ffn_half, "shard", axis=0, tiled=True),
    )
    ffn_vecs = (
        lax.psum_scatter(grad_up_bias, "shard", scatter_dimension=0, tiled=True),
        lax.psum_scatter(grad_down_bias, "shard", scatter_dimension=0, tiled=True),
        lax.psum_scatter(grad_ffn_gain, "shard", scatter_dimension=0, tiled=True),
        lax.psum_scatter(grad_ffn_shift, "shard", scatter_dimension=0, tiled=True),
    )
    ffn_shares = (
        contract_rows(mid_cols, pre_group),
        ffn_vecs[0],
        contract_rows(hidden_cols, ffn_group),
        ffn_vecs[1],
        ffn_vecs[2],
        ffn_vecs[3],
    )
    grad_attn_shift = jnp.sum(grad_mid, axis=0)
    grad_attn_gain = jnp.sum(grad_mid * normed_one, axis=0)
    grad_attn_sum = norm_backward(
        grad_mid, normed_one, inverse_one, attn_gain_full.astype(jnp.float32)
    )
    attn_half = grad_attn_sum.astype(jnp.bfloat16)
    grad_proj_bias = jnp.sum(grad_attn_sum, axis=0)
    grad_context = times_transposed(attn_half, proj_full).astype(jnp.bfloat16)
    grad_query, grad_key, grad_value = attention_backward(
        query_rows, key_rows, value_rows, log_total, lengths, grad_context
    )
    grad_query_bias = jnp.sum(grad_query, axis=0)
    grad_value_bias = jnp.sum(grad_value, axis=0)
    grad_packed = jnp.concatenate([grad_query, grad_key, grad_value], axis=1).astype(jnp.bfloat16)
    grad_tokens = (grad_attn_sum + times_transposed(grad_packed, qkv_full)).astype(jnp.bfloat16)
    packed_group, attn_group = (
        lax.all_gather(grad_packed, "shard", axis=0, tiled=True),
        lax.all_gather(attn_half, "shard", axis=0, tiled=True),
    )
    attn_vecs = (
        lax.psum_scatter(grad_query_bias, "shard", scatter_dimension=0, tiled=True),
        lax.psum_scatter(grad_value_bias, "shard", scatter_dimension=0, tiled=True),
        lax.psum_scatter(grad_proj_bias, "shard", scatter_dimension=0, tiled=True),
        lax.psum_scatter(grad_attn_gain, "shard", scatter_dimension=0, tiled=True),
        lax.psum_scatter(grad_attn_shift, "shard", scatter_dimension=0, tiled=True),
    )
    attn_shares = (
        contract_rows(token_cols, packed_group),
        attn_vecs[0],
        attn_vecs[1],
        contract_rows(context_cols, attn_group),
        attn_vecs[2],
        attn_vecs[3],
        attn_vecs[4],
    )
    summed = (
        lax.psum(attn_shares[0].astype(jnp.bfloat16), "rep").astype(jnp.float32),
        lax.psum(attn_shares[1].astype(jnp.bfloat16), "rep").astype(jnp.float32),
        lax.psum(attn_shares[2].astype(jnp.bfloat16), "rep").astype(jnp.float32),
        lax.psum(attn_shares[3].astype(jnp.bfloat16), "rep").astype(jnp.float32),
        lax.psum(attn_shares[4].astype(jnp.bfloat16), "rep").astype(jnp.float32),
        lax.psum(attn_shares[5].astype(jnp.bfloat16), "rep").astype(jnp.float32),
        lax.psum(attn_shares[6].astype(jnp.bfloat16), "rep").astype(jnp.float32),
        lax.psum(ffn_shares[0].astype(jnp.bfloat16), "rep").astype(jnp.float32),
        lax.psum(ffn_shares[1].astype(jnp.bfloat16), "rep").astype(jnp.float32),
        lax.psum(ffn_shares[2].astype(jnp.bfloat16), "rep").astype(jnp.float32),
        lax.psum(ffn_shares[3].astype(jnp.bfloat16), "rep").astype(jnp.float32),
        lax.psum(ffn_shares[4].astype(jnp.bfloat16), "rep").astype(jnp.float32),
        lax.psum(ffn_shares[5].astype(jnp.bfloat16), "rep").astype(jnp.float32),
    )
    return (
        layer_output,
        grad_tokens,
        summed[0],
        summed[1],
        summed[2],
        summed[3],
        summed[4],
        summed[5],
        summed[6],
        summed[7],
        summed[8],
        summed[9],
        summed[10],
        summed[11],
        summed[12],
    )


def solution(mesh):
    placed = (
        P(("rep", "shard"), None),
        P(("rep", "shard")),
        P("shard", None),
        P("shard"),
        P("shard"),
        P("shard", None),
        P("shard"),
        P("shard"),
        P("shard"),
        P("shard", None),
        P("shard"),
        P("shard", None),
        P("shard"),
        P("shard"),
        P("shard"),
        P(("rep", "shard"), None),
    )
    return jax.shard_map(
        per_device,
        mesh=mesh,
        in_specs=placed,
        out_specs=(
            P(("rep", "shard"), None),
            P(("rep", "shard"), None),
            P("shard", None),
            P("shard"),
            P("shard"),
            P("shard", None),
            P("shard"),
            P("shard"),
            P("shard"),
            P("shard", None),
            P("shard"),
            P("shard", None),
            P("shard"),
            P("shard"),
            P("shard"),
        ),
        check_vma=False,
    )
```

profile of v0, /device:TPU:0, one launch (start us, length us, event | category | flops | bytes accessed | tf_op | source)
XLA Modules:
  0.0 712.5 jit_solution(2446243803208572598)
XLA Ops:
  10.1 5.3 all-gather.5
  15.5 4.4 all_gather.59
  19.9 4.4 all-gather.2
  24.2 4.6 all-gather.1
  28.8 4.5 all-gather
  34.1 4.5 all-gather.4
  38.6 4.5 all-gather.3
  43.2 4.5 all-gather.6
  47.8 4.5 all-gather.7
  52.3 40.6 %all-gather.15.cloned.1.call-done = bf16[1024,3072]{1,0:T(8,128)(2,1)} async-done(((bf16[512,3072]{1,0:T(8,128)(2,1)}), bf16[1024,3072]{1,0:T(8,128)(2,1)}) %all-gather.15.cloned.1.call-update) | async-done | bytes 6291472 | tf_op jit(solution)/shard_map/all_gather | solution.py:118
  92.9 3.8 fusion.58
  98.2 29.3 %all-gather.17.cloned.1.call-done = bf16[1024,1024]{1,0:T(8,128)(2,1)} async-done(((bf16[512,1024]{1,0:T(8,128)(2,1)}), bf16[1024,1024]{1,0:T(8,128)(2,1)}) %all-gather.17.cloned.1.call-update) | async-done | bytes 2097168 | tf_op jit(solution)/shard_map/all_gather | solution.py:121
  131.5 101.7 %all-gather.19.cloned.1.call-done = bf16[1024,4096]{1,0:T(8,128)(2,1)} async-done(((bf16[512,4096]{1,0:T(8,128)(2,1)}), bf16[1024,4096]{1,0:T(8,128)(2,1)}) %all-gather.19.cloned.1.call-update) | async-done | bytes 8388624 | tf_op jit(solution)/shard_map/all_gather | solution.py:152
  233.1 6.3 multiply_convert_fusion
  239.5 99.1 %all-gather.21.cloned.1.call-done = bf16[4096,1024]{1,0:T(8,128)(2,1)} async-done(((bf16[2048,1024]{1,0:T(8,128)(2,1)}), bf16[4096,1024]{1,0:T(8,128)(2,1)}) %all-gather.21.cloned.1.call-update) | async-done | bytes 8388624 | tf_op jit(solution)/shard_map/all_gather | solution.py:154
  338.6 4.9 fusion.55
  348.6 6.8 multiply_reduce_fusion.1
  376.5 4.4 all-to-all-done
  380.9 3.4 all-to-all-start.1
  386.2 6.8 all-to-all-done.1
  393.0 3.6 all-to-all-start.3
  396.6 23.8 %all_gather.65 = bf16[256,1024]{1,0:T(8,128)(2,1)S(1)} all-gather(bf16[128,1024]{1,0:T(8,128)(2,1)S(1)} %convert_element_type.198), channel_id=1, replica_groups=mesh['rep'=16,'shard'=2] {'shard'}, dimensions={0}, use_global_device_ids=true | all-gather | bytes 786432 | tf_op jit(solution)/shard_map/all_gather | solution.py:225
  420.4 14.4 %all_gather.67 = bf16[256,1024]{1,0:T(8,128)(2,1)S(1)} all-gather(bf16[128,1024]{1,0:T(8,128)(2,1)S(1)} %copy-done.10), channel_id=1, replica_groups=mesh['rep'=16,'shard'=2] {'shard'}, dimensions={0}, use_global_device_ids=true | all-gather | bytes 786432 | tf_op jit(solution)/shard_map/all_gather | solution.py:192
  443.0 4.1 fusion.2
  448.6 4.9 convolution_convert_fusion
  456.2 7.5 %all-reduce.9 = (bf16[1024]{0:T(1024)(128)(2,1)S(1)}, bf16[1024]{0:T(1024)(128)(2,1)S(1)}, bf16[1024]{0:T(1024)(128)(2,1)S(1)}, bf16[1024]{0:T(1024)(128)(2,1)S(...) all-reduce(f32[1024]{0:T(1024)S(1)} %reduce_sum.186, ...), channel_id=2, replica_groups=mesh['rep'=16,'shard'=2] {'shard'}, use_global_device_ids=true, to_apply=%region_12.13.clone | all-reduce | flops 12288 | bytes 73728
  464.3 63.1 %all-reduce.10 = (bf16[512]{0:T(512)(128)(2,1)S(1)}, bf16[512]{0:T(512)(128)(2,1)S(1)}, bf16[512]{0:T(512)(128)(2,1)S(1)}, bf16[512]{0:T(512)(128)(2,1)S(1)}, bf...) all-reduce(bf16[512]{0:T(512)(128)(2,1)S(1)} %dynamic-slice.35, ...), channel_id=1, replica_groups=mesh['rep'=16,'shard'=2] {'rep'}, use_global_device_ids=true, to_apply=%region_13.14 | all-reduce | flops 6144 | bytes 24576 | tf_op jit(solution)/shard_map/psum | solution.py:245
  532.6 5.8 fusion.16
  538.4 148.9 %all-reduce.14.cloned.1.call-done = (bf16[512,3072]{0,1:T(8,128)(2,1)}, bf16[512,1024]{1,0:T(8,128)(2,1)}, bf16[512,4096]{1,0:T(8,128)(2,1)}, bf16[2048,1024]{1,0:T(8,128)(2,1)}) async-done(((bf16[512,3072]{0,1:T(8,128)(2,1)}, bf16[512,1024]{1,0:T(8,128)(2,1)}, bf16[512,4096]{1,0:T(8,128)(2,1)}, bf16[2048,1024]{1,0:T(8,128)(2,1)}), (bf16[512,3072]{0,1:T(8,128)(2,1)}, bf16[512,1024]{1,0:T(8,128)(2,1)}, ...) | async-done | bytes 12582928 | tf_op jit(solution)/shard_map/psum | solution.py:244
  687.3 5.5 copy.83
  694.4 6.8 convert_element_type.219
  701.2 4.4 convert_element_type.223
  (168 shorter events, 54.6 us)
Async XLA Ops:
  7.2 85.7 %all-gather.15.cloned.1.call-start = ((), (), s32[]{:S(2)}) async-start(), calls=%async_computation.4 | async-start | bytes 9437184 | tf_op jit(solution)/shard_map/all_gather | solution.py:118
  7.9 119.7 %all-gather.17.cloned.1.call-start = ((), (), s32[]{:S(2)}) async-start(), calls=%async_computation.5 | async-start | bytes 3145728 | tf_op jit(solution)/shard_map/all_gather | solution.py:121
  8.7 224.5 %all-gather.19.cloned.1.call-start = ((), (), s32[]{:S(2)}) async-start(), calls=%async_computation.6 | async-start | bytes 12582912 | tf_op jit(solution)/shard_map/all_gather | solution.py:152
  9.4 10.4 %copy-start.24 = (bf16[512]{0:T(512)(128)(2,1)S(1)}, bf16[512]{0:T(512)(128)(2,1)}, u32[]{:S(2)}) copy-start(bf16[512]{0:T(512)(128)(2,1)} %param.22) | copy-start | bytes 3076
  9.4 14.8 %copy-start.25 = (bf16[512]{0:T(512)(128)(2,1)S(1)}, bf16[512]{0:T(512)(128)(2,1)}, u32[]{:S(2)}) copy-start(bf16[512]{0:T(512)(128)(2,1)} %param.19) | copy-start | bytes 3076
  9.4 19.4 %copy-start.26 = (bf16[512]{0:T(512)(128)(2,1)S(1)}, bf16[512]{0:T(512)(128)(2,1)}, u32[]{:S(2)}) copy-start(bf16[512]{0:T(512)(128)(2,1)} %param.20) | copy-start | bytes 3076
  9.5 24.6 %copy-start.27 = (bf16[512]{0:T(512)(128)(2,1)S(1)}, bf16[512]{0:T(512)(128)(2,1)}, u32[]{:S(2)}) copy-start(bf16[512]{0:T(512)(128)(2,1)} %param.24) | copy-start | bytes 3076
  9.5 29.1 %copy-start.28 = (bf16[512]{0:T(512)(128)(2,1)S(1)}, bf16[512]{0:T(512)(128)(2,1)}, u32[]{:S(2)}) copy-start(bf16[512]{0:T(512)(128)(2,1)} %param.23) | copy-start | bytes 3076
  9.5 33.7 %copy-start.29 = (bf16[512]{0:T(512)(128)(2,1)S(1)}, bf16[512]{0:T(512)(128)(2,1)}, u32[]{:S(2)}) copy-start(bf16[512]{0:T(512)(128)(2,1)} %param.29) | copy-start | bytes 3076
  9.5 38.3 %copy-start.30 = (bf16[512]{0:T(512)(128)(2,1)S(1)}, bf16[512]{0:T(512)(128)(2,1)}, u32[]{:S(2)}) copy-start(bf16[512]{0:T(512)(128)(2,1)} %param.30) | copy-start | bytes 3076
  9.5 83.4 %copy-start.3 = (bf16[128,1024]{1,0:T(8,128)(2,1)S(1)}, bf16[128,1024]{1,0:T(8,128)(2,1)}, u32[]{:S(2)}) copy-start(bf16[128,1024]{1,0:T(8,128)(2,1)} %param.16) | copy-start | bytes 786436
  9.5 329.1 %all-gather.21.cloned.1.call-start = ((), (), s32[]{:S(2)}) async-start(), calls=%async_computation.7 | async-start | bytes 12582912 | tf_op jit(solution)/shard_map/all_gather | solution.py:154
  10.1 433.0 %all-gather.23.cloned.1.call-start = ((), (), s32[]{:S(2)}) async-start(), calls=%async_computation.8 | async-start | bytes 2359296 | tf_op jit(solution)/shard_map/all_gather | solution.py:224
  97.2 30.4 %copy-start.15 = (bf16[128,1024]{0,1:T(8,128)(2,1)}, bf16[128,1024]{0,1:T(8,128)(2,1)S(1)}, u32[]{:S(2)}) copy-start(bf16[128,1024]{0,1:T(8,128)(2,1)S(1)} %copy.71) | copy-start | bytes 786436
  97.4 32.4 %copy-start.12 = (bf16[128,1024]{0,1:T(8,128)(2,1)}, bf16[128,1024]{0,1:T(8,128)(2,1)S(1)}, u32[]{:S(2)}) copy-start(bf16[128,1024]{0,1:T(8,128)(2,1)S(1)} %copy.72) | copy-start | bytes 786436
  97.7 32.4 %copy-start.11 = (f32[16,128,128]{1,2,0:T(8,128)}, f32[16,128,128]{1,2,0:T(8,128)S(1)}, u32[]{:S(2)}) copy-start(f32[16,128,128]{1,2,0:T(8,128)S(1)} %convolution_multiply_fusion.1) | copy-start | bytes 3145732
  98.2 31.7 %copy-start.17 = (bf16[16,64,128]{2,1,0:T(8,128)(2,1)}, bf16[16,64,128]{2,1,0:T(8,128)(2,1)S(1)}, u32[]{:S(2)}) copy-start(bf16[16,64,128]{2,1,0:T(8,128)(2,1)S(1)} %convolution_convert_fusion.6) | copy-start | bytes 786436
  130.1 109.3 %copy-start.4 = (bf16[128,1024]{1,0:T(8,128)(2,1)}, bf16[128,1024]{1,0:T(8,128)(2,1)S(1)}, u32[]{:S(2)}) copy-start(bf16[128,1024]{1,0:T(8,128)(2,1)S(1)} %fusion.36) | copy-start | bytes 786436
  358.8 7.2 %copy-start.13 = (bf16[128,1024]{0,1:T(8,128)(2,1)S(1)}, bf16[128,1024]{0,1:T(8,128)(2,1)}, u32[]{:S(2)}) copy-start(bf16[128,1024]{0,1:T(8,128)(2,1)} %copy-done.12) | copy-start | bytes 786436
  368.6 7.0 copy-start.18
  370.7 13.8 %copy-start.5 = (bf16[128,1024]{1,0:T(8,128)(2,1)S(1)}, bf16[128,1024]{1,0:T(8,128)(2,1)}, u32[]{:S(2)}) copy-start(bf16[128,1024]{1,0:T(8,128)(2,1)} %copy-done.4) | copy-start | bytes 786436
  370.7 77.9 %all-gather.25.cloned.1.call-start = ((), (), s32[]{:S(2)}) async-start(), calls=%async_computation.9 | async-start | bytes 3145728 | tf_op jit(solution)/shard_map/all_gather | solution.py:191
  372.2 8.7 %all-to-all-start = ((bf16[128,2,512]{0,2,1:T(8,128)(2,1)}), bf16[128,2,512]{0,2,1:T(8,128)(2,1)S(1)}, u32[]{:S(2)}, u32[]{:S(2)}) async-start(bf16[128,2,512]{0,2,1:T(8,128)(2,1)} %bitcast.25), calls=%async_computation | async-start | bytes 524288 | tf_op jit(solution)/shard_map/all_to_all | solution.py:173
  380.9 12.1 %all-to-all-start.1 = ((bf16[128,2,512]{2,0,1:T(8,128)(2,1)}), bf16[128,2,512]{2,0,1:T(8,128)(2,1)S(1)}, u32[]{:S(2)}, u32[]{:S(2)}) async-start(bf16[128,2,512]{2,0,1:T(8,128)(2,1)} %copy.80), calls=%async_computation.1 | async-start | bytes 524288 | tf_op jit(solution)/shard_map/all_to_all | solution.py:174
  385.2 35.2 %copy-start.10 = (bf16[128,1024]{1,0:T(8,128)(2,1)S(1)}, bf16[128,1024]{1,0:T(8,128)(2,1)}, u32[]{:S(2)}) copy-start(bf16[128,1024]{1,0:T(8,128)(2,1)} %copy-done.9) | copy-start | bytes 786436
  393.0 43.2 %all-to-all-start.3 = ((bf16[128,2,2048]{2,0,1:T(8,128)(2,1)}), bf16[128,2,2048]{2,0,1:T(8,128)(2,1)S(1)}, u32[]{:S(2)}, u32[]{:S(2)}) async-start(bf16[128,2,2048]{2,0,1:T(8,128)(2,1)} %bitcast.87), calls=%async_computation.3 | async-start | bytes 2097152 | tf_op jit(solution)/shard_map/all_to_all | solution.py:176
  436.2 11.5 %all-to-all-start.2 = ((bf16[128,2,512]{2,0,1:T(8,128)(2,1)}), bf16[128,2,512]{2,0,1:T(8,128)(2,1)S(1)}, u32[]{:S(2)}, u32[]{:S(2)}) async-start(bf16[128,2,512]{2,0,1:T(8,128)(2,1)} %bitcast.88), calls=%async_computation.2 | async-start | bytes 524288 | tf_op jit(solution)/shard_map/all_to_all | solution.py:175
  439.7 247.7 %all-reduce.14.cloned.1.call-start = ((), (), s32[]{:S(2)}) async-start(), calls=%async_computation.10 | async-start | bytes 25165824 | tf_op jit(solution)/shard_map/psum | solution.py:244
  453.5 79.1 %copy-start.19 = (bf16[1,128,16,64]{1,3,2,0:T(8,128)(2,1)S(1)}, bf16[1,128,16,64]{1,3,2,0:T(8,128)(2,1)}, u32[]{:S(2)}) copy-start(bf16[1,128,16,64]{1,3,2,0:T(8,128)(2,1)} %get-tuple-element.115) | copy-start | bytes 786436
  453.5 79.1 %copy-start.20 = (bf16[16,64,128]{2,1,0:T(8,128)(2,1)S(1)}, bf16[16,64,128]{2,1,0:T(8,128)(2,1)}, u32[]{:S(2)}) copy-start(bf16[16,64,128]{2,1,0:T(8,128)(2,1)} %convolution_convert_fusion.4) | copy-start | bytes 786436
  453.5 79.1 %copy-start.21 = (bf16[1,128,16,64]{1,3,2,0:T(8,128)(2,1)S(1)}, bf16[1,128,16,64]{1,3,2,0:T(8,128)(2,1)}, u32[]{:S(2)}) copy-start(bf16[1,128,16,64]{1,3,2,0:T(8,128)(2,1)} %get-tuple-element.117) | copy-start | bytes 786436
  694.4 6.8 copy-start.1
  (13 other events, 46.9 us)
Sparse Core Ops, SparseCore 0:
  9.5 83.3 all-gather.14
  94.4 33.1 all-gather.16
  129.1 103.9 all-gather.18
  234.5 103.9 all-gather.20
  370.9 32.3 all-gather.22
  404.6 43.9 all-gather.24
  454.3 232.9 all-reduce.13
where the time goes:
time: 714 us; the launch traced here: 712 us
  waiting for transfers between devices  435 us (61%)
  blocking collectives  150 us (21%)
  matrix products  58.3 us (8%)
  other arithmetic  23.7 us (3%)
  between operations  16.7 us (2%)
  starting transfers between devices  14.2 us (2%)
  local copies, waits for them, and re-layouts  14.2 us (2%)
    psum x1, waiting for transfers between devices, per_device(): lax.psum(attn_shares[0].astype(jnp.bfloat16), 'rep').astype(jnp.float32)  149 us
    all_gather x1, waiting for transfers between devices, per_device(): lax.all_gather(up_weight, 'shard', axis=0, tiled=True)  102 us
    all_gather x1, waiting for transfers between devices, per_device(): lax.all_gather(down_weight, 'shard', axis=0, tiled=True)  99.1 us
    psum x1, blocking collectives, per_device(): lax.psum(attn_shares[1].astype(jnp.bfloat16), 'rep').astype(jnp.float32)  63.1 us
    all_gather x1, waiting for transfers between devices, per_device(): lax.all_gather(qkv_weight, 'shard', axis=0, tiled=True)  40.6 us
    all_gather x1, waiting for transfers between devices, per_device(): lax.all_gather(proj_weight, 'shard', axis=0, tiled=True)  29.3 us
    all_gather x1, blocking collectives, per_device(): lax.all_gather(attn_half, 'shard', axis=0, tiled=True)  23.8 us
    dot_general x4, matrix products, times_transposed(): lax.dot_general(former, latter, (((1,), (1,)), ((), ())), preferred_eleme...  16.7 us
  transfers between devices with their start and end apart: 11, of which 9 were waited for; matrix products, arithmetic and copies ran while one was open for 6% of the time, Pallas kernels for 0%

commit v1 on v0

--- a/solution.py
+++ b/solution.py
@@ -9,6 +9,18 @@
 EPSILON = 1e-05
 SQRT_HALF = 0.7071067811865476
 INV_ROOT_TAU = 0.3989422804014327
+
+
+def doubled_up(value, axis, dim):
+    ways, here, turn = (lax.axis_size(axis), lax.axis_index(axis), value.shape[dim])
+    line, have = (value, 1)
+    while have < ways:
+        line = jnp.concatenate(
+            [line, lax.ppermute(line, axis, [(d, (d - have) % ways) for d in range(ways)])],
+            axis=dim,
+        )
+        have = 2 * have
+    return jnp.roll(line, here * turn, axis=dim)
 
 
 def gelu_value(pre_act):
@@ -149,7 +161,7 @@
     )
     mid_half = mid_state.astype(jnp.bfloat16)
     up_full, up_bias_full, down_full, down_bias_full, ffn_gain_full, ffn_shift_full = (
-        lax.all_gather(up_weight, "shard", axis=0, tiled=True),
+        doubled_up(up_weight, "shard", 0),
         lax.all_gather(up_bias, "shard", axis=0, tiled=True),
         lax.all_gather(down_weight, "shard", axis=0, tiled=True),
         lax.all_gather(down_bias, "shard", axis=0, tiled=True),

time: 714 us -> 676 us (0.947)
  waiting for transfers between devices: 435 us -> 228 us
  blocking collectives: 150 us -> 303 us
  other arithmetic: 23.7 us -> 37.5 us
    all_gather x1, blocking collectives: 5.32 us -> 158 us  [per_device(): lax.all_gather(down_bias, 'shard', axis=0, tiled=True)]
    all_gather x1 -> x0, waiting for transfers between devices: 102 us -> none  [per_device(): lax.all_gather(up_weight, 'shard', axis=0, tiled=True)]
    all_gather x1, waiting for transfers between devices: 40.6 us -> 0.01 us  [per_device(): lax.all_gather(qkv_weight, 'shard', axis=0, tiled=True)]
    all_gather x1, waiting for transfers between devices: 99.1 us -> 64.3 us  [per_device(): lax.all_gather(down_weight, 'shard', axis=0, tiled=True)]
    all_gather x1, waiting for transfers between devices: 29.3 us -> 0.02 us  [per_device(): lax.all_gather(proj_weight, 'shard', axis=0, tiled=True)]
    concatenate x0 -> x1, other arithmetic: none -> 13.8 us  [doubled_up(): return jnp.roll(line, here * turn, axis=dim)]
  transfers between devices with their start and end apart: 11 -> 11, of which waited for: 9 -> 6; matrix products, arithmetic and copies ran while one was open for 6% -> 8% of each run, Pallas kernels for 0% -> 0%
where the time goes in v1:
time: 676 us; the launch traced here: 675 us
  blocking collectives  303 us (45%)
  waiting for transfers between devices  228 us (34%)
  matrix products  58.4 us (9%)
  other arithmetic  37.5 us (6%)
  starting transfers between devices  17.2 us (3%)
  between operations  16.7 us (2%)
  local copies, waits for them, and re-layouts  14.2 us (2%)
    all_gather x1, blocking collectives, per_device(): lax.all_gather(down_bias, 'shard', axis=0, tiled=True)  158 us
    psum x1, waiting for transfers between devices, per_device(): lax.psum(attn_shares[0].astype(jnp.bfloat16), 'rep').astype(jnp.float32)  149 us
    all_gather x1, waiting for transfers between devices, per_device(): lax.all_gather(down_weight, 'shard', axis=0, tiled=True)  64.3 us
    psum x1, blocking collectives, per_device(): lax.psum(attn_shares[1].astype(jnp.bfloat16), 'rep').astype(jnp.float32)  63 us
    all_gather x1, blocking collectives, per_device(): lax.all_gather(attn_half, 'shard', axis=0, tiled=True)  23.8 us
    dot_general x4, matrix products, times_transposed(): lax.dot_general(former, latter, (((1,), (1,)), ((), ())), preferred_eleme...  16.9 us
    all_gather x1, blocking collectives, per_device(): lax.all_gather(ffn_half, 'shard', axis=0, tiled=True)  14.4 us
    concatenate x1, other arithmetic, doubled_up(): return jnp.roll(line, here * turn, axis=dim)  13.8 us
  transfers between devices with their start and end apart: 11, of which 6 were waited for; matrix products, arithmetic and copies ran while one was open for 8% of the time, Pallas kernels for 0%

profile of v1, /device:TPU:0, one launch (start us, length us, event | category | flops | bytes accessed | tf_op | source)
XLA Modules:
  0.0 674.5 jit_solution(16786547974147117627)
XLA Ops:
  12.0 158.3 %all-gather.5 = bf16[2,1,512]{2,1,0:T(2,128)(2,1)S(1)} all-gather(bf16[1,1,512]{2,1,0:T(2,128)(2,1)S(1)} %reshape.213), channel_id=1, replica_groups=mesh['rep'=16,'shard'=2] {'shard'}, dimensions={0}, use_global_device_ids=true | all-gather | bytes 3072 | tf_op jit(solution)/shard_map/all_gather | solution.py:167
  170.2 4.6 all_gather.55
  174.8 4.5 all-gather.2
  179.4 4.6 all-gather.1
  184.0 4.4 all-gather
  189.1 4.5 all-gather.4
  193.6 4.4 all-gather.3
  198.0 4.4 all-gather.6
  202.4 4.4 all-gather.7
  206.8 13.8 %fusion.4 = bf16[1024,4096]{1,0:T(8,128)(2,1)} fusion(s32[]{:T(128)S(6)} %select_n.26, bf16[512,4096]{1,0:T(8,128)(2,1)} %param.25, bf16[512,4096]{1,0:T(8,128)(2,1)} %collective-permute-done), kind=kLoop, calls=%fused_computation.8 | loop fusion | flops 33554432 | bytes 16777220 | tf_op jit(solution)/shard_map/jit(_roll_dynamic)/concatenate | solution.py:23
  220.7 3.8 fusion.61
  230.0 6.3 multiply_convert_fusion
  236.3 64.3 %all-gather.18.cloned.1.call-done = bf16[4096,1024]{1,0:T(8,128)(2,1)} async-done(((bf16[2048,1024]{1,0:T(8,128)(2,1)}), bf16[4096,1024]{1,0:T(8,128)(2,1)}) %all-gather.18.cloned.1.call-update) | async-done | bytes 8388624 | tf_op jit(solution)/shard_map/all_gather | solution.py:166
  300.7 4.9 fusion.58
  307.5 3.4 fusion.54
  310.9 6.8 %multiply_reduce_fusion.1 = (f32[1024]{0:T(1024)S(1)}, f32[128]{0:T(128)S(1)}, f32[128]{0:T(128)S(1)}, f32[1024]{0:T(1024)S(1)}, f32[128,1024]{1,0:T(8,128)S(1)}) fusion(f32[128,1024]{1,0:T(8,128)S(1)} %get-tuple-element.119, f32[128]{0:T(128)S(1)} %add_rsqrt_fusion.1, f32[128]{0:T(128)S(1)} %broadcast_multiply_fusion.5, f32[1024]{0:T(1024)S(1)} %bitcast.117, ...), kind=kOutput, calls=%fused_computation.64 | convolution fusion | flops 1075050240 | bytes 11024384 | tf_op jit(solution)/shard_map/dot_general | solution.py:58
  334.4 3.4 all-to-all-start
  338.7 4.4 all-to-all-done
  343.1 3.4 all-to-all-start.1
  348.4 6.8 %all-to-all-done.1 = bf16[128,2,512]{2,0,1:T(8,128)(2,1)S(1)} async-done(((bf16[128,2,512]{2,0,1:T(8,128)(2,1)}), bf16[128,2,512]{2,0,1:T(8,128)(2,1)S(1)}, u32[]{:S(2)}, u32[]{:S(2)}) %all-to-all-start.1) | async-done | bytes 262176 | tf_op jit(solution)/shard_map/all_to_all | solution.py:186
  355.2 3.6 all-to-all-start.3
  358.8 23.8 %all_gather.61 = bf16[256,1024]{1,0:T(8,128)(2,1)S(1)} all-gather(bf16[128,1024]{1,0:T(8,128)(2,1)S(1)} %convert_element_type.198), channel_id=1, replica_groups=mesh['rep'=16,'shard'=2] {'shard'}, dimensions={0}, use_global_device_ids=true | all-gather | bytes 786432 | tf_op jit(solution)/shard_map/all_gather | solution.py:237
  382.6 14.4 %all_gather.63 = bf16[256,1024]{1,0:T(8,128)(2,1)S(1)} all-gather(bf16[128,1024]{1,0:T(8,128)(2,1)S(1)} %copy-done.10), channel_id=1, replica_groups=mesh['rep'=16,'shard'=2] {'shard'}, dimensions={0}, use_global_device_ids=true | all-gather | bytes 786432 | tf_op jit(solution)/shard_map/all_gather | solution.py:204
  405.2 4.0 fusion.5
  410.8 4.9 convolution_convert_fusion
  418.4 7.5 %all-reduce.9 = (bf16[1024]{0:T(1024)(128)(2,1)S(1)}, bf16[1024]{0:T(1024)(128)(2,1)S(1)}, bf16[1024]{0:T(1024)(128)(2,1)S(1)}, bf16[1024]{0:T(1024)(128)(2,1)S(...) all-reduce(f32[1024]{0:T(1024)S(1)} %reduce_sum.186, ...), channel_id=2, replica_groups=mesh['rep'=16,'shard'=2] {'shard'}, use_global_device_ids=true, to_apply=%region_12.13.clone | all-reduce | flops 12288 | bytes 73728
  426.5 63.0 %all-reduce.10 = (bf16[512]{0:T(512)(128)(2,1)S(1)}, bf16[512]{0:T(512)(128)(2,1)S(1)}, bf16[512]{0:T(512)(128)(2,1)S(1)}, bf16[512]{0:T(512)(128)(2,1)S(1)}, bf...) all-reduce(bf16[512]{0:T(512)(128)(2,1)S(1)} %dynamic-slice.35, ...), channel_id=1, replica_groups=mesh['rep'=16,'shard'=2] {'rep'}, use_global_device_ids=true, to_apply=%region_13.14 | all-reduce | flops 6144 | bytes 24576 | tf_op jit(solution)/shard_map/psum | solution.py:257
  494.8 5.8 fusion.19
  500.6 148.8 %all-reduce.14.cloned.1.call-done = (bf16[512,3072]{0,1:T(8,128)(2,1)}, bf16[512,1024]{1,0:T(8,128)(2,1)}, bf16[512,4096]{1,0:T(8,128)(2,1)}, bf16[2048,1024]{1,0:T(8,128)(2,1)}) async-done(((bf16[512,3072]{0,1:T(8,128)(2,1)}, bf16[512,1024]{1,0:T(8,128)(2,1)}, bf16[512,4096]{1,0:T(8,128)(2,1)}, bf16[2048,1024]{1,0:T(8,128)(2,1)}), (bf16[512,3072]{0,1:T(8,128)(2,1)}, bf16[512,1024]{1,0:T(8,128)(2,1)}, ...) | async-done | bytes 12582928 | tf_op jit(solution)/shard_map/psum | solution.py:256
  649.4 5.5 copy.83
  656.4 6.8 %convert_element_type.219 = f32[512,4096]{1,0:T(8,128)} convert(bf16[512,4096]{1,0:T(8,128)(2,1)} %get-tuple-element.103) | non-fusion elementwise | flops 2097152 | bytes 12582912 | tf_op jit(solution)/shard_map/convert_element_type | solution.py:263
  663.3 4.4 convert_element_type.223
  (168 shorter events, 49.7 us)
Async XLA Ops:
  7.2 213.5 %all-gather.14.cloned.1.call-start = ((), (), s32[]{:S(2)}) async-start(), calls=%async_computation.4 | async-start | bytes 9437184 | tf_op jit(solution)/shard_map/all_gather | solution.py:130
  7.9 218.1 %all-gather.16.cloned.1.call-start = ((), (), s32[]{:S(2)}) async-start(), calls=%async_computation.5 | async-start | bytes 3145728 | tf_op jit(solution)/shard_map/all_gather | solution.py:133
  8.7 161.5 %copy-start.22 = (bf16[2048]{0:T(1024)(128)(2,1)S(1)}, bf16[2048]{0:T(1024)(128)(2,1)}, u32[]{:S(2)}) copy-start(bf16[2048]{0:T(1024)(128)(2,1)} %param.26) | copy-start | bytes 12292
  8.7 166.1 %copy-start.24 = (bf16[512]{0:T(512)(128)(2,1)S(1)}, bf16[512]{0:T(512)(128)(2,1)}, u32[]{:S(2)}) copy-start(bf16[512]{0:T(512)(128)(2,1)} %param.22) | copy-start | bytes 3076
  8.7 170.7 %copy-start.25 = (bf16[512]{0:T(512)(128)(2,1)S(1)}, bf16[512]{0:T(512)(128)(2,1)}, u32[]{:S(2)}) copy-start(bf16[512]{0:T(512)(128)(2,1)} %param.19) | copy-start | bytes 3076
  8.7 175.2 %copy-start.26 = (bf16[512]{0:T(512)(128)(2,1)S(1)}, bf16[512]{0:T(512)(128)(2,1)}, u32[]{:S(2)}) copy-start(bf16[512]{0:T(512)(128)(2,1)} %param.20) | copy-start | bytes 3076
  8.7 180.3 %copy-start.27 = (bf16[512]{0:T(512)(128)(2,1)S(1)}, bf16[512]{0:T(512)(128)(2,1)}, u32[]{:S(2)}) copy-start(bf16[512]{0:T(512)(128)(2,1)} %param.24) | copy-start | bytes 3076
  8.7 184.9 %copy-start.28 = (bf16[512]{0:T(512)(128)(2,1)S(1)}, bf16[512]{0:T(512)(128)(2,1)}, u32[]{:S(2)}) copy-start(bf16[512]{0:T(512)(128)(2,1)} %param.23) | copy-start | bytes 3076
  8.7 189.3 %copy-start.29 = (bf16[512]{0:T(512)(128)(2,1)S(1)}, bf16[512]{0:T(512)(128)(2,1)}, u32[]{:S(2)}) copy-start(bf16[512]{0:T(512)(128)(2,1)} %param.29) | copy-start | bytes 3076
  8.7 193.7 %copy-start.30 = (bf16[512]{0:T(512)(128)(2,1)S(1)}, bf16[512]{0:T(512)(128)(2,1)}, u32[]{:S(2)}) copy-start(bf16[512]{0:T(512)(128)(2,1)} %param.30) | copy-start | bytes 3076
  8.8 291.9 %all-gather.18.cloned.1.call-start = ((), (), s32[]{:S(2)}) async-start(), calls=%async_computation.6 | async-start | bytes 12582912 | tf_op jit(solution)/shard_map/all_gather | solution.py:166
  8.8 198.0 %collective-permute-start = (bf16[512,4096]{1,0:T(8,128)(2,1)}, bf16[512,4096]{1,0:T(8,128)(2,1)}, u32[]{:S(2)}, u32[]{:S(2)}) collective-permute-start(bf16[512,4096]{1,0:T(8,128)(2,1)} %param.25), channel_id=1, source_target_pairs={{0,1},{1,0},{2,3},{3,2},{4,5},{5,4},{6,7},{7,6},{8,9},{9,8},{10,11... | collective-permute-start | bytes 12582920 | tf_op jit(solution)/shard_map/ppermute | solution.py:19
  11.9 393.4 %all-gather.20.cloned.1.call-start = ((), (), s32[]{:S(2)}) async-start(), calls=%async_computation.7 | async-start | bytes 2359296 | tf_op jit(solution)/shard_map/all_gather | solution.py:236
  206.8 13.9 %copy-start.3 = (bf16[128,1024]{1,0:T(8,128)(2,1)S(1)}, bf16[128,1024]{1,0:T(8,128)(2,1)}, u32[]{:S(2)}) copy-start(bf16[128,1024]{1,0:T(8,128)(2,1)} %param.16) | copy-start | bytes 786436
  228.7 7.6 %copy-start.4 = (bf16[128,1024]{1,0:T(8,128)(2,1)}, bf16[128,1024]{1,0:T(8,128)(2,1)S(1)}, u32[]{:S(2)}) copy-start(bf16[128,1024]{1,0:T(8,128)(2,1)S(1)} %fusion.39) | copy-start | bytes 786436
  300.7 6.5 slice-start
  300.7 6.5 slice-start.1
  310.9 6.8 %copy-start.2 = (bf16[128,4096]{1,0:T(8,128)(2,1)}, bf16[128,4096]{1,0:T(8,128)(2,1)S(1)}, u32[]{:S(2)}) copy-start(bf16[128,4096]{1,0:T(8,128)(2,1)S(1)} %get-tuple-element.110) | copy-start | bytes 3145732
  321.1 7.1 %copy-start.13 = (bf16[128,1024]{0,1:T(8,128)(2,1)S(1)}, bf16[128,1024]{0,1:T(8,128)(2,1)}, u32[]{:S(2)}) copy-start(bf16[128,1024]{0,1:T(8,128)(2,1)} %copy-done.12) | copy-start | bytes 786436
  330.8 7.0 %copy-start.18 = (bf16[16,64,128]{2,1,0:T(8,128)(2,1)S(1)}, bf16[16,64,128]{2,1,0:T(8,128)(2,1)}, u32[]{:S(2)}) copy-start(bf16[16,64,128]{2,1,0:T(8,128)(2,1)} %copy-done.17) | copy-start | bytes 786436
  332.9 13.8 %copy-start.5 = (bf16[128,1024]{1,0:T(8,128)(2,1)S(1)}, bf16[128,1024]{1,0:T(8,128)(2,1)}, u32[]{:S(2)}) copy-start(bf16[128,1024]{1,0:T(8,128)(2,1)} %copy-done.4) | copy-start | bytes 786436
  332.9 77.9 %all-gather.22.cloned.1.call-start = ((), (), s32[]{:S(2)}) async-start(), calls=%async_computation.8 | async-start | bytes 3145728 | tf_op jit(solution)/shard_map/all_gather | solution.py:203
  334.4 8.7 %all-to-all-start = ((bf16[128,2,512]{0,2,1:T(8,128)(2,1)}), bf16[128,2,512]{0,2,1:T(8,128)(2,1)S(1)}, u32[]{:S(2)}, u32[]{:S(2)}) async-start(bf16[128,2,512]{0,2,1:T(8,128)(2,1)} %bitcast.25), calls=%async_computation | async-start | bytes 524288 | tf_op jit(solution)/shard_map/all_to_all | solution.py:185
  343.1 12.1 %all-to-all-start.1 = ((bf16[128,2,512]{2,0,1:T(8,128)(2,1)}), bf16[128,2,512]{2,0,1:T(8,128)(2,1)S(1)}, u32[]{:S(2)}, u32[]{:S(2)}) async-start(bf16[128,2,512]{2,0,1:T(8,128)(2,1)} %copy.80), calls=%async_computation.1 | async-start | bytes 524288 | tf_op jit(solution)/shard_map/all_to_all | solution.py:186
  347.4 35.2 %copy-start.10 = (bf16[128,1024]{1,0:T(8,128)(2,1)S(1)}, bf16[128,1024]{1,0:T(8,128)(2,1)}, u32[]{:S(2)}) copy-start(bf16[128,1024]{1,0:T(8,128)(2,1)} %copy-done.9) | copy-start | bytes 786436
  355.2 43.2 %all-to-all-start.3 = ((bf16[128,2,2048]{2,0,1:T(8,128)(2,1)}), bf16[128,2,2048]{2,0,1:T(8,128)(2,1)S(1)}, u32[]{:S(2)}, u32[]{:S(2)}) async-start(bf16[128,2,2048]{2,0,1:T(8,128)(2,1)} %bitcast.87), calls=%async_computation.3 | async-start | bytes 2097152 | tf_op jit(solution)/shard_map/all_to_all | solution.py:188
  398.4 11.5 %all-to-all-start.2 = ((bf16[128,2,512]{2,0,1:T(8,128)(2,1)}), bf16[128,2,512]{2,0,1:T(8,128)(2,1)S(1)}, u32[]{:S(2)}, u32[]{:S(2)}) async-start(bf16[128,2,512]{2,0,1:T(8,128)(2,1)} %bitcast.88), calls=%async_computation.2 | async-start | bytes 524288 | tf_op jit(solution)/shard_map/all_to_all | solution.py:187
  401.9 247.5 %all-reduce.14.cloned.1.call-start = ((), (), s32[]{:S(2)}) async-start(), calls=%async_computation.9 | async-start | bytes 25165824 | tf_op jit(solution)/shard_map/psum | solution.py:256
  415.7 79.1 %copy-start.19 = (bf16[1,128,16,64]{1,3,2,0:T(8,128)(2,1)S(1)}, bf16[1,128,16,64]{1,3,2,0:T(8,128)(2,1)}, u32[]{:S(2)}) copy-start(bf16[1,128,16,64]{1,3,2,0:T(8,128)(2,1)} %get-tuple-element.115) | copy-start | bytes 786436
  415.7 79.1 %copy-start.20 = (bf16[16,64,128]{2,1,0:T(8,128)(2,1)S(1)}, bf16[16,64,128]{2,1,0:T(8,128)(2,1)}, u32[]{:S(2)}) copy-start(bf16[16,64,128]{2,1,0:T(8,128)(2,1)} %convolution_convert_fusion.4) | copy-start | bytes 786436
  415.7 79.1 %copy-start.21 = (bf16[1,128,16,64]{1,3,2,0:T(8,128)(2,1)S(1)}, bf16[1,128,16,64]{1,3,2,0:T(8,128)(2,1)}, u32[]{:S(2)}) copy-start(bf16[1,128,16,64]{1,3,2,0:T(8,128)(2,1)} %get-tuple-element.117) | copy-start | bytes 786436
  656.4 6.8 %copy-start.1 = (bf16[2048,1024]{1,0:T(8,128)(2,1)S(1)}, bf16[2048,1024]{1,0:T(8,128)(2,1)}, u32[]{:S(2)}) copy-start(bf16[2048,1024]{1,0:T(8,128)(2,1)} %get-tuple-element.104) | copy-start | bytes 12582916
  (13 other events, 33.8 us)
Sparse Core Ops, SparseCore 0:
  9.5 150.5 all-gather.13
  161.7 33.3 all-gather.15
  196.7 103.9 all-gather.17
  333.1 32.3 all-gather.19
  366.8 43.9 all-gather.21
  416.4 232.9 all-reduce.13
